TPU v7x, 32 devices: a whole 2x2x4 slice. The times are simulated.
32 devices in a mesh: seq: 8 (over z, y), head: 4 (over x, core).
Axes of the slice: x: 2, y: 2, z: 4, core: 2. Of those that a mesh axis runs over, the one named last changes fastest.
Arguments:
- tokens: bfloat16 [1024, 2048], P('seq'), may hold values from -20 to 20, as said below
- projection: bfloat16 [2048, 3072], P(None, 'head'), may hold values from -0.078125 to 0.078125
- context_cotangent: bfloat16 [1024, 2048], P('seq', 'head'), may hold values from -80 to 80
Outputs:
- perturbed_context: bfloat16 [1024, 2048], P('seq', 'head')
- ascent_direction: float32 [2048, 3072], P('seq', 'head')
Inputs may be any that keep to these rules, and one draw needn't show every extreme that they name: `tokens`: activations of the layer.
All inputs are finite; a program needn't handle non-finite values.
Results may differ from a plain program's by a relative error of at most 0.017.
Values may be sent and summed in bfloat16 or wider, within the bound.
A program may use at most 64 MiB of HBM per device.

v0:
```python
import math
import jax
import jax.numpy as jnp
from jax import lax
from jax.sharding import PartitionSpec as P

INPUT_FEATURES = 2048
KEY_VALUE_HEADS = 4
HEAD_DIMENSION = 128
QUERY_PER_GROUP = 4
masked_score = -1e30
key_block = 512


def attend_fold(query_rows, query_pos, score_scale):
    head_size = query_rows.shape[1]

    def single_block(carry_state, block_rows, offset):
        running_max, row_total, context_sum = carry_state
        key_rows = block_rows[:, :head_size]
        value_rows = block_rows[:, head_size:].astype(jnp.float32)
        scores = jnp.dot(query_rows, key_rows.T, preferred_element_type=jnp.float32) * score_scale
        key_pos = offset + jnp.arange(block_rows.shape[0], dtype=jnp.int32)
        allowed = key_pos[None, :] <= query_pos[:, None]
        scores = jnp.where(allowed, scores, masked_score)
        new_max = jnp.maximum(running_max, jnp.max(scores, axis=1))
        factor = jnp.exp(running_max - new_max)
        weights = jnp.where(allowed, jnp.exp(scores - new_max[:, None]), 0.0)
        row_total = row_total * factor + jnp.sum(weights, axis=1)
        context_sum = context_sum * factor[:, None] + jnp.dot(
            weights, value_rows, precision=lax.Precision.HIGHEST, preferred_element_type=jnp.float32
        )
        return (new_max, row_total, context_sum)

    def fold_keys(carry_state, block_rows, offset):
        row_count = block_rows.shape[0]
        if row_count > key_block and row_count % key_block == 0:

            def sub_block(block_index, inner_state):
                part_rows = lax.dynamic_slice_in_dim(
                    block_rows, block_index * key_block, key_block, 0
                )
                return single_block(inner_state, part_rows, block_index * key_block)

            return lax.fori_loop(0, row_count // key_block, sub_block, carry_state)
        return single_block(carry_state, block_rows, offset)

    return fold_keys


def on_device(tokens, projection, context_cotangent):
    score_scale = HEAD_DIMENSION ** (-0.5)
    local_rows = tokens.shape[0]
    rows_all = local_rows * QUERY_PER_GROUP
    first_row = lax.axis_index("seq") * local_rows
    query_pos = first_row + jnp.arange(rows_all, dtype=jnp.int32) // QUERY_PER_GROUP

    def split_heads(projected_weight):
        reshaped_grads = projected_weight.reshape(local_rows, QUERY_PER_GROUP + 2, HEAD_DIMENSION)
        query_rows = reshaped_grads[:, :QUERY_PER_GROUP].reshape(rows_all, HEAD_DIMENSION)
        key_value = reshaped_grads[:, QUERY_PER_GROUP:].reshape(local_rows, 2 * HEAD_DIMENSION)
        return (query_rows, key_value)

    def empty_state():
        return (
            jnp.full((rows_all,), masked_score, jnp.float32),
            jnp.zeros((rows_all,), jnp.float32),
            jnp.zeros((rows_all, HEAD_DIMENSION), jnp.float32),
        )

    projected_weight = jnp.dot(tokens, projection, preferred_element_type=jnp.float32).astype(
        jnp.bfloat16
    )
    query_rows, key_value = split_heads(projected_weight)
    gathered = lax.all_gather(key_value, "seq", axis=0, tiled=True)
    total_rows = gathered.shape[0]
    block_size = min(key_block, total_rows)
    needed = (first_row + local_rows - 1) // block_size + 1
    fold_first = attend_fold(query_rows, query_pos, score_scale)

    def forward_step(block_index, carry_state):
        block_rows = lax.dynamic_slice_in_dim(gathered, block_index * block_size, block_size, 0)
        return fold_first(carry_state, block_rows, block_index * block_size)

    running_max, row_total, context_sum = lax.fori_loop(0, needed, forward_step, empty_state())
    context = (context_sum / row_total[:, None]).astype(jnp.bfloat16)
    log_total = running_max + jnp.log(row_total)
    grad_rows = context_cotangent.reshape(rows_all, HEAD_DIMENSION)
    row_delta = jnp.sum(grad_rows.astype(jnp.float32) * context.astype(jnp.float32), axis=1)
    contract_rows = (((0,), (0,)), ((), ()))

    def backward_step(block_index, carry_state):
        query_grad, key_terms = carry_state
        offset = block_index * block_size
        block_rows = lax.dynamic_slice_in_dim(gathered, offset, block_size, 0)
        key_rows = block_rows[:, :HEAD_DIMENSION]
        value_rows = block_rows[:, HEAD_DIMENSION:]
        scores = jnp.dot(query_rows, key_rows.T, preferred_element_type=jnp.float32) * score_scale
        key_pos = offset + jnp.arange(block_size, dtype=jnp.int32)
        allowed = key_pos[None, :] <= query_pos[:, None]
        probs_full = jnp.where(allowed, jnp.exp(scores - log_total[:, None]), 0.0)
        probs_half = probs_full.astype(jnp.bfloat16)
        prob_grad = jnp.dot(grad_rows, value_rows.T, preferred_element_type=jnp.float32)
        score_grad = (probs_full * (prob_grad - row_delta[:, None]) * score_scale).astype(
            jnp.bfloat16
        )
        query_grad = query_grad + jnp.dot(score_grad, key_rows, preferred_element_type=jnp.float32)
        key_grad = lax.dot_general(
            score_grad, query_rows, contract_rows, preferred_element_type=jnp.float32
        )
        value_grad = lax.dot_general(
            probs_half, grad_rows, contract_rows, preferred_element_type=jnp.float32
        )
        key_terms = lax.dynamic_update_slice_in_dim(
            key_terms, jnp.concatenate([key_grad, value_grad], axis=1), offset, 0
        )
        return (query_grad, key_terms)

    initial = (
        jnp.zeros((rows_all, HEAD_DIMENSION), jnp.float32),
        jnp.zeros((total_rows, 2 * HEAD_DIMENSION), jnp.float32),
    )
    query_grad, key_terms = lax.fori_loop(0, needed, backward_step, initial)
    key_value_grad = lax.psum_scatter(key_terms, "seq", scatter_dimension=0, tiled=True).astype(
        jnp.bfloat16
    )
    head_grads = jnp.concatenate(
        [
            query_grad.astype(jnp.bfloat16).reshape(local_rows, QUERY_PER_GROUP * HEAD_DIMENSION),
            key_value_grad,
        ],
        axis=1,
    )
    grad_term = lax.dot_general(
        tokens, head_grads, contract_rows, preferred_element_type=jnp.float32
    )
    normalizing_scale = math.sqrt(
        INPUT_FEATURES * KEY_VALUE_HEADS * (QUERY_PER_GROUP + 2) * HEAD_DIMENSION
    )
    ascent_radius = 0.2 * math.sqrt(KEY_VALUE_HEADS * (QUERY_PER_GROUP + 2) * HEAD_DIMENSION)
    weight_grad = lax.psum(grad_term, "seq")
    square_sum = lax.psum(jnp.sum(weight_grad * weight_grad), "head")
    grad_norm = jnp.sqrt(square_sum)
    share_rows = INPUT_FEATURES // lax.axis_size("seq")
    own_grad = lax.dynamic_slice_in_dim(
        weight_grad, lax.axis_index("seq") * share_rows, share_rows, 0
    )
    direction = own_grad * (normalizing_scale / grad_norm)
    moved_weights = (
        projection.astype(jnp.float32) + ascent_radius / grad_norm * weight_grad
    ).astype(jnp.bfloat16)
    projected_new = jnp.dot(tokens, moved_weights, preferred_element_type=jnp.float32).astype(
        jnp.bfloat16
    )
    query_new, key_value_new = split_heads(projected_new)
    fold_new = attend_fold(query_new, query_pos, score_scale)
    final_state = fold_new(
        empty_state(), lax.all_gather(key_value_new, "seq", axis=0, tiled=True), jnp.int32(0)
    )
    perturbed = (
        (final_state[2] / final_state[1][:, None])
        .astype(jnp.bfloat16)
        .reshape(local_rows, QUERY_PER_GROUP * HEAD_DIMENSION)
    )
    return (perturbed, direction)


def solution(mesh):
    return jax.shard_map(
        on_device,
        mesh=mesh,
        in_specs=(P("seq", None), P(None, "head"), P("seq", "head")),
        out_specs=(P("seq", "head"), P("seq", "head")),
        check_vma=False,
    )
```

profile of v0, /device:TPU:0, one launch (start us, length us, event | category | flops | bytes accessed | tf_op | source)
XLA Modules:
  0.0 397.3 jit_solution(14726550498906386122)
XLA Ops:
  7.2 1.0 copy-done
  8.2 2.5 convolution_convert_fusion
  11.0 33.0 %all_gather.6 = bf16[1024,256]{1,0:T(8,128)(2,1)S(1)} all-gather(bf16[128,256]{1,0:T(8,128)(2,1)S(1)} %copy.22), channel_id=1, replica_groups=mesh['seq'=8,'head'=4] {'seq'}, dimensions={0}, use_global_device_ids=true | all-gather | bytes 589824 | tf_op jit(solution)/shard_map/all_gather | solution.py:75
  44.2 1.8 while.46
  44.9 1.2 convolution_add_fusion.6
  46.4 1.1 broadcast_in_dim.50
  47.6 2.6 while.47
  47.6 0.4 fusion.120
  48.9 0.9 maximum_dynamic-update-slice_fusion.2
  50.3 70.2 %reduce-scatter.2.cloned.1.call-done = f32[128,256]{0,1:T(8,128)} async-done(((f32[1024,256]{0,1:T(8,128)}), f32[128,256]{0,1:T(8,128)}) %reduce-scatter.2.cloned.1.call-update) | async-done | bytes 131088 | tf_op jit(solution)/shard_map/reduce_scatter | solution.py:124
  120.6 0.9 convert_element_type.49
  121.6 3.7 convolution_bitcast_fusion
  125.3 4.7 %copy.20 = bf16[2048,768]{0,1:T(8,128)(2,1)} copy(bf16[2048,768]{1,0:T(8,128)(2,1)} %param.10) | data formatting | bytes 6291456 | tf_op args[1]
  130.0 204.6 %all-reduce.2.cloned.1.call-done = f32[2048,768]{0,1:T(8,128)} async-done(((f32[2048,768]{0,1:T(8,128)}), f32[2048,768]{0,1:T(8,128)}) %all-reduce.2.cloned.1.call-update) | async-done | bytes 6291472 | tf_op jit(solution)/shard_map/psum | solution.py:141
  334.6 5.0 %multiply_reduce_fusion = f32[]{:T(128)} fusion(f32[2048,768]{0,1:T(8,128)} %all-reduce.2.cloned.1.call-done), kind=kLoop, calls=%fused_computation.85 | loop fusion | flops 3145727 | bytes 6291460 | tf_op jit(solution)/shard_map/reduce_sum | solution.py:142
  339.6 6.8 %psum.15 = f32[]{:T(128)} all-reduce(f32[]{:T(128)} %multiply_reduce_fusion), channel_id=1, replica_groups=mesh['seq'=8,'head'=4] {'head'}, use_global_device_ids=true, to_apply=%region_10.11 | all-reduce | flops 1 | bytes 8 | tf_op jit(solution)/shard_map/psum | solution.py:142
  347.2 4.7 %fusion.58 = bf16[768,128]{1,0:T(8,128)(2,1)S(1)} fusion(bf16[128,2048]{1,0:T(8,128)(2,1)S(1)} %copy-done, f32[2048,768]{0,1:T(8,128)} %all-reduce.2.cloned.1.call-done, bf16[2048,768]{0,1:T(8,128)(2,1)} %copy.20, f32[]{:T(128)S(6)} %div.45), kind=kOutput, calls=%fused_computation.89 | convolution fusion | flops 409042944 | bytes 10158084 | tf_op jit(solution)/shard_map/dot_general | solution.py:152
  352.0 1.2 dynamic-slice_multiply_fusion
  353.2 1.1 copy.27
  354.4 31.3 %all_gather.7 = bf16[1024,256]{1,0:T(8,128)(2,1)S(1)} all-gather(bf16[128,256]{1,0:T(8,128)(2,1)S(1)} %copy.28), channel_id=1, replica_groups=mesh['seq'=8,'head'=4] {'seq'}, dimensions={0}, use_global_device_ids=true | all-gather | bytes 589824 | tf_op jit(solution)/shard_map/all_gather | solution.py:158
  385.9 3.6 while.48
  386.5 1.2 convolution_add_fusion.8
  388.3 1.2 convolution_add_fusion.8
  389.7 0.7 reshape.62
  (53 shorter events, 4.6 us)
Async XLA Ops:
  7.2 1.0 copy-start
  7.2 113.4 %reduce-scatter.2.cloned.1.call-start = ((), (), s32[]{:S(2)}) async-start(), calls=%async_computation.1 | async-start | bytes 1179648 | tf_op jit(solution)/shard_map/reduce_scatter | solution.py:124
  44.2 1.8 copy-start.1
  50.2 284.5 %all-reduce.2.cloned.1.call-start = ((), (), s32[]{:S(2)}) async-start(), calls=%async_computation.2 | async-start | bytes 12582912 | tf_op jit(solution)/shard_map/psum | solution.py:141
Sparse Core Ops, SparseCore 0:
  50.3 70.2 reduce-scatter.1
  125.4 209.1 all-reduce.1
where the time goes:
time: 398 us; the launch traced here: 397 us
  waiting for transfers between devices  275 us (69%)
  blocking collectives  71.2 us (18%)
  matrix products  16.9 us (4%)
  between operations  15 us (4%)
  local copies, waits for them, and re-layouts  9.76 us (2%)
  other arithmetic  9.18 us (2%)
    psum x1, waiting for transfers between devices, on_device(): weight_grad = lax.psum(grad_term, 'seq')  205 us
    reduce_scatter x1, waiting for transfers between devices, on_device(): lax.psum_scatter(key_terms, 'seq', scatter_dimension=0, tiled=True)  70.2 us
    all_gather x1, blocking collectives, on_device(): gathered = lax.all_gather(key_value, 'seq', axis=0, tiled=True)  33 us
    all_gather x1, blocking collectives, on_device(): lax.all_gather(key_value_new, 'seq', axis=0, tiled=True)  31.3 us
  transfers between devices with their start and end apart: 2, of which 2 were waited for; matrix products, arithmetic and copies ran while one was open for 1% of the time, Pallas kernels for 0%

commit v1 on v0

--- a/solution.py
+++ b/solution.py
@@ -138,7 +138,11 @@
         INPUT_FEATURES * KEY_VALUE_HEADS * (QUERY_PER_GROUP + 2) * HEAD_DIMENSION
     )
     ascent_radius = 0.2 * math.sqrt(KEY_VALUE_HEADS * (QUERY_PER_GROUP + 2) * HEAD_DIMENSION)
-    weight_grad = lax.psum(grad_term, "seq")
+    weight_grad = grad_term
+    for hop in (1, 2, 4):
+        weight_grad = weight_grad + lax.ppermute(
+            weight_grad, "seq", [(dev, dev ^ hop) for dev in range(8)]
+        )
     square_sum = lax.psum(jnp.sum(weight_grad * weight_grad), "head")
     grad_norm = jnp.sqrt(square_sum)
     share_rows = INPUT_FEATURES // lax.axis_size("seq")

time: 398 us -> 738 us (1.85)
  waiting for transfers between devices: 275 us -> 602 us
  other arithmetic: 9.18 us -> 20.2 us
    ppermute x0 -> x3, waiting for transfers between devices: none -> 532 us  [on_device(): lax.ppermute(weight_grad, 'seq', [(dev, dev ^ hop) for dev in range(8)])]
    psum x1 -> x0, waiting for transfers between devices: 205 us -> none  [on_device(): weight_grad = lax.psum(grad_term, 'seq')]
  transfers between devices with their start and end apart: 2 -> 4, of which waited for: 2 -> 4; matrix products, arithmetic and copies ran while one was open for 1% -> 1% of each run, Pallas kernels for 0% -> 0%
where the time goes in v1:
time: 738 us; the launch traced here: 737 us
  waiting for transfers between devices  602 us (82%)
  blocking collectives  72.1 us (10%)
  other arithmetic  20.2 us (3%)
  between operations  15 us (2%)
  matrix products  14.3 us (2%)
  local copies, waits for them, and re-layouts  9.75 us (1%)
    ppermute x3, waiting for transfers between devices, on_device(): lax.ppermute(weight_grad, 'seq', [(dev, dev ^ hop) for dev in range(8)])  532 us
    reduce_scatter x1, waiting for transfers between devices, on_device(): lax.psum_scatter(key_terms, 'seq', scatter_dimension=0, tiled=True)  70.2 us
    all_gather x1, blocking collectives, on_device(): gathered = lax.all_gather(key_value, 'seq', axis=0, tiled=True)  33 us
    all_gather x1, blocking collectives, on_device(): lax.all_gather(key_value_new, 'seq', axis=0, tiled=True)  31.4 us
  transfers between devices with their start and end apart: 4, of which 4 were waited for; matrix products, arithmetic and copies ran while one was open for 1% of the time, Pallas kernels for 0%

profile of v1, /device:TPU:0, one launch (start us, length us, event | category | flops | bytes accessed | tf_op | source)
XLA Modules:
  0.0 737.2 jit_solution(11627710627217491548)
XLA Ops:
  8.2 2.5 convolution_convert_fusion
  11.0 33.0 %all_gather.6 = bf16[1024,256]{1,0:T(8,128)(2,1)S(1)} all-gather(bf16[128,256]{1,0:T(8,128)(2,1)S(1)} %copy.22), channel_id=1, replica_groups=mesh['seq'=8,'head'=4] {'seq'}, dimensions={0}, use_global_device_ids=true | all-gather | bytes 589824 | tf_op jit(solution)/shard_map/all_gather | solution.py:75
  44.2 1.8 while.46
  44.9 1.2 convolution_add_fusion.6
  46.4 1.1 broadcast_in_dim.50
  47.6 2.6 while.47
  50.3 70.2 %reduce-scatter.2.cloned.1.call-done = f32[128,256]{0,1:T(8,128)} async-done(((f32[1024,256]{0,1:T(8,128)}), f32[128,256]{0,1:T(8,128)}) %reduce-scatter.2.cloned.1.call-update) | async-done | bytes 131088 | tf_op jit(solution)/shard_map/reduce_scatter | solution.py:124
  122.6 1.2 collective-permute-start
  123.7 134.4 %collective-permute-done = f32[2048,768]{0,1:T(8,128)S(1)} collective-permute-done((f32[2048,768]{0,1:T(8,128)S(1)}, f32[2048,768]{0,1:T(8,128)S(1)}, u32[]{:S(2)}, u32[]{:S(2)}) %collective-permute-start) | collective-permute-done | bytes 6291488 | tf_op jit(solution)/shard_map/ppermute | solution.py:143
  258.1 1.9 add.136
  260.0 1.1 collective-permute-start.1
  261.1 133.5 %collective-permute-done.1 = f32[2048,768]{0,1:T(8,128)S(1)} collective-permute-done((f32[2048,768]{0,1:T(8,128)S(1)}, f32[2048,768]{0,1:T(8,128)S(1)}, u32[]{:S(2)}, u32[]{:S(2)}) %collective-permute-start.1) | collective-permute-done | bytes 6291488 | tf_op jit(solution)/shard_map/ppermute | solution.py:143
  394.7 4.0 add.137
  399.7 4.7 copy.20
  404.4 264.0 %collective-permute-done.2 = f32[2048,768]{0,1:T(8,128)} collective-permute-done((f32[2048,768]{0,1:T(8,128)}, f32[2048,768]{0,1:T(8,128)}, u32[]{:S(2)}, u32[]{:S(2)}) %collective-permute-start.2) | collective-permute-done | bytes 6291488 | tf_op jit(solution)/shard_map/ppermute | solution.py:143
  668.4 10.2 %multiply_reduce_fusion = (f32[]{:T(128)}, f32[2048,768]{0,1:T(8,128)}) fusion(f32[2048,768]{0,1:T(8,128)} %add.137, f32[2048,768]{0,1:T(8,128)} %collective-permute-done.2), kind=kLoop, calls=%fused_computation.85 | loop fusion | flops 4718591 | bytes 18874372 | tf_op jit(solution)/shard_map/reduce_sum | solution.py:146
  678.6 7.7 %psum.7 = f32[]{:T(128)} all-reduce(f32[]{:T(128)} %get-tuple-element.364), channel_id=1, replica_groups=mesh['seq'=8,'head'=4] {'head'}, use_global_device_ids=true, to_apply=%region_9.10 | all-reduce | flops 1 | bytes 8 | tf_op jit(solution)/shard_map/psum | solution.py:146
  687.1 4.7 fusion.58
  691.8 1.2 dynamic-slice_multiply_fusion
  693.0 1.1 copy.27
  694.3 31.4 %all_gather.7 = bf16[1024,256]{1,0:T(8,128)(2,1)S(1)} all-gather(bf16[128,256]{1,0:T(8,128)(2,1)S(1)} %copy.28), channel_id=1, replica_groups=mesh['seq'=8,'head'=4] {'seq'}, dimensions={0}, use_global_device_ids=true | all-gather | bytes 589824 | tf_op jit(solution)/shard_map/all_gather | solution.py:162
  725.8 3.6 while.48
  726.5 1.2 convolution_add_fusion.8
  728.3 1.2 convolution_add_fusion.8
  (58 shorter events, 10.5 us)
Async XLA Ops:
  7.2 1.0 copy-start
  7.2 113.4 %reduce-scatter.2.cloned.1.call-start = ((), (), s32[]{:S(2)}) async-start(), calls=%async_computation.1 | async-start | bytes 1179648 | tf_op jit(solution)/shard_map/reduce_scatter | solution.py:124
  44.2 1.8 copy-start.1
  122.6 135.5 %collective-permute-start = (f32[2048,768]{0,1:T(8,128)S(1)}, f32[2048,768]{0,1:T(8,128)S(1)}, u32[]{:S(2)}, u32[]{:S(2)}) collective-permute-start(f32[2048,768]{0,1:T(8,128)S(1)} %convolution_bitcast_fusion), channel_id=1, source_target_pairs={{0,4},{4,0},{8,12},{12,8},{16,20},{20,16},{24,28},{28,24},{1,5},{5... | collective-permute-start | bytes 18874376 | tf_op jit(solution)/shard_map/ppermute | solution.py:143
  260.0 134.7 %collective-permute-start.1 = (f32[2048,768]{0,1:T(8,128)S(1)}, f32[2048,768]{0,1:T(8,128)S(1)}, u32[]{:S(2)}, u32[]{:S(2)}) collective-permute-start(f32[2048,768]{0,1:T(8,128)S(1)} %add.136), channel_id=1, source_target_pairs={{0,8},{4,12},{8,0},{12,4},{16,24},{20,28},{24,16},{28,20},{1,9},{5... | collective-permute-start | bytes 18874376 | tf_op jit(solution)/shard_map/ppermute | solution.py:143
  398.6 269.8 %collective-permute-start.2 = (f32[2048,768]{0,1:T(8,128)}, f32[2048,768]{0,1:T(8,128)}, u32[]{:S(2)}, u32[]{:S(2)}) collective-permute-start(f32[2048,768]{0,1:T(8,128)} %add.137), channel_id=1, source_target_pairs={{0,16},{4,20},{8,24},{12,28},{16,0},{20,4},{24,8},{28,12},{1,17},{... | collective-permute-start | bytes 18874376 | tf_op jit(solution)/shard_map/ppermute | solution.py:143
Sparse Core Ops, SparseCore 0:
  50.3 70.1 reduce-scatter.1
